TPU v7x, 32 devices: a whole 2x2x4 slice. The times are simulated.
32 devices in a mesh: req: 16 (over z, y, x), tp: 2 (over core).
Axes of the slice: x: 2, y: 2, z: 4, core: 2. Of those that a mesh axis runs over, the one named last changes fastest.
Arguments:
- tokens: bfloat16 [2048, 2560], P('req'), may hold values from -6 to 6
- input_norm_gain: bfloat16 [2560], replicated, may hold values from 0.5 to 1.5
- query_weight: bfloat16 [2560, 4096], P(None, 'tp'), may hold values from -0.125 to 0.125
- key_value_weight: bfloat16 [2, 2560, 1024], P(None, None, 'tp'), may hold values from -0.125 to 0.125
- query_head_gain: bfloat16 [128], replicated, may hold values from 0.25 to 1.75
- key_head_gain: bfloat16 [128], replicated, may hold values from 0.25 to 1.75
- adapter_down_maps: bfloat16 [16, 48, 2560], P('req', None, 'tp'), may hold values from -0.125 to 0.125
- query_up_maps: bfloat16 [16, 16, 4096], P('req', None, 'tp'), may hold values from -0.75 to 0.75
- key_value_up_maps: bfloat16 [16, 2, 16, 1024], P('req', None, None, 'tp'), may hold values from -0.75 to 0.75
- packed_lengths: int32 [4], replicated, may hold values from 64 to 1024, as said below
- adapter_per_prompt: int32 [4], replicated, may hold values from 0 to 15, as said below
- adapter_place: int32 [16], replicated, may hold values from 0 to 15, each once
Outputs:
- attended: bfloat16 [2048, 4096], P('req', 'tp')
Inputs may be any that keep to these rules, and one draw needn't show every extreme that they name: `packed_lengths`: every entry is a multiple of 64; exactly one is 1024, at least one is 64, and they sum to 2048. `adapter_per_prompt`: the prompts use distinct adapters.
All inputs are finite; a program needn't handle non-finite values.
Results may differ from a plain program's by a relative error of at most 0.0086.
Values may be sent and summed in bfloat16 or wider, within the bound.
A program may use at most 128 MiB of HBM per device.

v0:
```python
import math

import jax
import jax.numpy as jnp
from jax import lax
from jax.sharding import PartitionSpec as P

SHORT_LEN = 64


epsilon = 1e-06
theta = 1000000.0
adapter_scale = 2.0


def normalize(values, gain_vec):
    values = values.astype(jnp.float32)
    inverse = lax.rsqrt(jnp.mean(values * values, axis=-1, keepdims=True) + epsilon)
    return values * inverse * gain_vec.astype(jnp.float32)


def rotate(values, offsets):
    half_dim = values.shape[-1] // 2
    powers = jnp.arange(half_dim, dtype=jnp.float32) * (2.0 / values.shape[-1])
    frequency = theta ** (-powers)
    angles = offsets.astype(jnp.float32)[:, None] * frequency[None, :]
    cosine = jnp.cos(angles)[:, None, :]
    sine_part = jnp.sin(angles)[:, None, :]
    former = values[..., :half_dim]
    latter = values[..., half_dim:]
    return jnp.concatenate(
        [former * cosine - latter * sine_part, latter * cosine + former * sine_part], axis=-1
    )


def doc_start(positions, packed_lengths):
    doc_end = jnp.cumsum(packed_lengths)
    return jnp.sum(
        jnp.where(doc_end[None, :] <= positions[:, None], packed_lengths[None, :], 0), axis=1
    )


def holders(positions, packed_lengths, adapter_per_prompt, adapter_place):
    doc_end = jnp.cumsum(packed_lengths)
    inside = (doc_end[None, :] > positions[:, None]) & (
        doc_end[None, :] - packed_lengths[None, :] <= positions[:, None]
    )
    adapter = jnp.sum(jnp.where(inside, adapter_per_prompt[None, :], 0), axis=1)
    catalog = jnp.arange(adapter_place.shape[0], dtype=jnp.int32)
    return jnp.sum(
        jnp.where(adapter[:, None] == catalog[None, :], adapter_place[None, :], 0), axis=1
    )


def on_device(
    tokens,
    input_norm_gain,
    query_weight,
    key_value_weight,
    query_head_gain,
    key_head_gain,
    adapter_down_maps,
    query_up_maps,
    key_value_up_maps,
    packed_lengths,
    adapter_per_prompt,
    adapter_place,
):
    token_rows = tokens.shape[0]
    first_row = lax.axis_index("req") * token_rows
    positions = first_row + jnp.arange(token_rows, dtype=jnp.int32)
    starts = doc_start(positions, packed_lengths)
    owners = holders(positions, packed_lengths, adapter_per_prompt, adapter_place)
    unit_count = token_rows // SHORT_LEN
    unit_owner = owners[::SHORT_LEN]
    normed = normalize(tokens, input_norm_gain).astype(jnp.bfloat16)
    plain_query = jnp.dot(normed, query_weight, preferred_element_type=jnp.float32)
    plain_pair = jnp.einsum(
        "td,cdk->ctk", normed, key_value_weight, preferred_element_type=jnp.float32
    )
    rank_width = query_up_maps.shape[1]
    local_width = adapter_down_maps.shape[2]
    own_cols = lax.dynamic_slice_in_dim(normed, lax.axis_index("tp") * local_width, local_width, 1)
    pieces = (
        lax.all_gather(adapter_down_maps, "req", axis=0, tiled=True),
        lax.all_gather(query_up_maps, "req", axis=0, tiled=True),
        lax.all_gather(key_value_up_maps, "req", axis=0, tiled=True),
    )
    piece_count = pieces[0].shape[0]
    slots_here = jnp.arange(piece_count, dtype=jnp.int32)
    chosen = (unit_owner[:, None] == slots_here[None, :]).astype(jnp.bfloat16)
    down_sel = jnp.einsum(
        "uk,krd->urd", chosen, pieces[0], preferred_element_type=jnp.float32
    ).astype(jnp.bfloat16)
    upq_sel = jnp.einsum(
        "uk,krc->urc", chosen, pieces[1], preferred_element_type=jnp.float32
    ).astype(jnp.bfloat16)
    upkv_sel = jnp.einsum(
        "uk,kcrd->ucrd", chosen, pieces[2], preferred_element_type=jnp.float32
    ).astype(jnp.bfloat16)
    partial_sum = jnp.einsum(
        "utd,urd->utr",
        own_cols.reshape(unit_count, SHORT_LEN, local_width),
        down_sel,
        preferred_element_type=jnp.float32,
    )
    reduced_rank = lax.psum(partial_sum, "tp").astype(jnp.bfloat16)
    query_increment = jnp.einsum(
        "utr,urc->utc", reduced_rank[..., :rank_width], upq_sel, preferred_element_type=jnp.float32
    ).reshape(token_rows, -1)
    pair_rank = reduced_rank[..., rank_width:].reshape(unit_count, SHORT_LEN, 2, rank_width)
    pair_increment = jnp.einsum(
        "utcr,ucrk->cutk", pair_rank, upkv_sel, preferred_element_type=jnp.float32
    ).reshape(2, token_rows, -1)
    head_width = query_head_gain.shape[0]
    query_heads = query_weight.shape[1] // head_width
    key_value_heads = key_value_weight.shape[2] // head_width
    group_width = query_heads // key_value_heads
    offsets = positions - starts
    query_rotated = (plain_query + adapter_scale * query_increment).reshape(
        token_rows, query_heads, head_width
    )
    query_rotated = rotate(normalize(query_rotated, query_head_gain), offsets).astype(jnp.bfloat16)
    query_every_token = query_rotated.reshape(token_rows, key_value_heads, group_width, head_width)
    key_rotated = (plain_pair[0] + adapter_scale * pair_increment[0]).reshape(
        token_rows, key_value_heads, head_width
    )
    key_rotated = rotate(normalize(key_rotated, key_head_gain), offsets).astype(jnp.bfloat16)
    value_every_token = (
        (plain_pair[1] + adapter_scale * pair_increment[1])
        .reshape(token_rows, key_value_heads, head_width)
        .astype(jnp.bfloat16)
    )
    key_value = jnp.stack([key_rotated, value_every_token], axis=1)
    start_sums = (
        jnp.zeros((token_rows, key_value_heads, group_width), jnp.float32),
        jnp.zeros((token_rows, key_value_heads, group_width, head_width), jnp.float32),
    )
    segment = lax.all_gather(key_value, "req", axis=0, tiled=True)
    length_now = segment.shape[0]
    key_rows = max(
        (size_try for size_try in range(1, min(length_now, 1024) + 1) if length_now % size_try == 0)
    )
    block_count = length_now // key_rows
    blocks = segment.reshape(block_count, key_rows, 2, key_value_heads, head_width)
    block_first = jnp.int32(0) + key_rows * jnp.arange(block_count, dtype=jnp.int32)

    def key_step(running, block_entry):
        key_block, block_start = block_entry
        key_pos = block_start + jnp.arange(key_rows, dtype=jnp.int32)
        key_start = doc_start(key_pos, packed_lengths)
        visible = (
            (key_start[None, :] == starts[:, None])
            & (key_pos[None, :] <= positions[:, None])
            & (key_pos[None, :] >= 0)
        )
        scores = jnp.einsum(
            "tkgd,skd->tkgs", query_every_token, key_block[:, 0], preferred_element_type=jnp.float32
        ) / math.sqrt(head_width)
        weights = jnp.where(visible[:, None, None, :], jnp.exp(scores), 0.0)
        totals = running[0] + jnp.sum(weights, axis=-1)
        numerator = running[1] + jnp.einsum(
            "tkgs,skd->tkgd",
            weights.astype(jnp.bfloat16),
            key_block[:, 1],
            preferred_element_type=jnp.float32,
        )
        return ((totals, numerator), None)

    result = lax.scan(key_step, start_sums, (blocks, block_first))[0]
    output_rows = result[1] / result[0][..., None]
    return output_rows.reshape(token_rows, query_heads * head_width).astype(jnp.bfloat16)


def solution(mesh):
    in_specs = (
        P("req", None),
        P(),
        P(None, "tp"),
        P(None, None, "tp"),
        P(),
        P(),
        P("req", None, "tp"),
        P("req", None, "tp"),
        P("req", None, None, "tp"),
        P(),
        P(),
        P(),
    )
    out_specs = P("req", "tp")
    return jax.shard_map(
        on_device, mesh=mesh, in_specs=in_specs, out_specs=out_specs, check_vma=False
    )
```

profile of v0, /device:TPU:16, one launch (start us, length us, event | category | flops | bytes accessed | tf_op | source)
XLA Modules:
  0.0 243.7 jit_solution(10807951525644673926)
XLA Ops:
  6.5 0.7 all-gather.4.cloned.1.call-update
  7.3 0.0 all-gather.8.cloned.1.call-start
  7.3 0.7 all-gather.8.cloned.1.call-update
  8.0 0.0 all-gather.6.cloned.1.call-start
  8.1 0.8 reduce-window.9
  8.9 0.7 bitcast_subtract_fusion
  9.6 35.8 %all_gather.13 = bf16[16,2,16,512]{3,2,1,0:T(8,128)(2,1)S(1)} all-gather(bf16[1,2,16,512]{3,2,1,0:T(8,128)(2,1)} %param.22), channel_id=1, replica_groups=mesh['req'=16,'tp'=2] {'req'}, dimensions={0}, use_global_device_ids=true | all-gather | bytes 557056 | tf_op jit(solution)/shard_map/all_gather | solution.py:87
  45.4 0.8 select_reduce_fusion.2
  46.1 0.7 select_reduce_fusion.1
  46.9 0.1 slice.44
  47.0 0.7 convert_element_type.67
  47.7 1.3 fusion.20
  49.0 1.3 fusion.22
  50.4 3.3 %convolution_bitcast_fusion = f32[2,128,512]{2,1,0:T(8,128)S(1)} fusion(bf16[2,2560,512]{2,1,0:T(8,128)(2,1)} %param.17, bf16[128,2560]{1,0:T(8,128)(2,1)S(1)} %fusion.22), kind=kOutput, calls=%fused_computation.33 | convolution fusion | flops 671088640 | bytes 6422528 | tf_op jit(solution)/shard_map/td,cdk->ctk/dot_general | solution.py:78
  53.7 0.1 squeeze.27
  53.9 0.1 squeeze.26
  54.0 0.4 convolution_convert_fusion.2
  54.4 0.3 multiply_cosine_fusion
  54.7 16.7 %all-gather.4.cloned.1.call-done = bf16[16,48,1280]{2,1,0:T(8,128)(2,1)} async-done(((bf16[1,48,1280]{2,1,0:T(8,128)(2,1)}), bf16[16,48,1280]{2,1,0:T(8,128)(2,1)}) %all-gather.4.cloned.1.call-update) | async-done | bytes 1966096 | tf_op jit(solution)/shard_map/all_gather | solution.py:85
  71.4 2.3 convolution_convert_fusion
  73.7 0.2 fusion.27
  73.9 3.7 %psum.7 = bf16[2,64,48]{1,2,0:T(8,128)(2,1)S(1)} all-reduce(f32[2,64,48]{1,2,0:T(8,128)S(1)} %fusion.27), channel_id=1, replica_groups=mesh['req'=16,'tp'=2] {'tp'}, use_global_device_ids=true, to_apply=%region_4.5 | all-reduce | flops 6144 | bytes 36864 | tf_op jit(solution)/shard_map/psum | solution.py:107
  77.6 0.3 fusion.32
  77.9 0.1 mul.221
  78.0 0.1 mul.204
  78.1 0.1 multiply_reduce_fusion.1
  78.3 0.1 multiply_multiply_fusion.1
  78.4 0.1 fusion.29
  78.6 0.8 pad_maximum_fusion.1
  79.4 0.0 all-gather.6.cloned.1.call-update
  79.5 0.2 broadcast_in_dim.65
  79.6 47.7 %all-gather.8.cloned.1.call-done = bf16[16,16,2048]{2,1,0:T(8,128)(2,1)} async-done(((bf16[1,16,2048]{2,1,0:T(8,128)(2,1)}), bf16[16,16,2048]{2,1,0:T(8,128)(2,1)}) %all-gather.8.cloned.1.call-update) | async-done | bytes 1048592 | tf_op jit(solution)/shard_map/all_gather | solution.py:86
  127.4 2.4 %convolution_convert_fusion.1 = bf16[2,16,2048]{2,0,1:T(2,128)(2,1)S(1)} fusion(bf16[16,16,2048]{2,1,0:T(8,128)(2,1)} %all-gather.8.cloned.1.call-done, s32[2]{0:T(128)S(1)} %slice.44), kind=kOutput, calls=%fused_computation.25 | convolution fusion | flops 2162720 | bytes 1179656 | tf_op jit(solution)/shard_map/uk,krc->urc/dot_general | solution.py:95
  129.8 0.3 convolution_multiply_fusion
  130.2 5.5 %fusion.19 = f32[16,8,16,128]{3,1,2,0:T(8,128)S(1)} fusion(f32[128,2048]{1,0:T(8,128)S(1)} %bitcast.99, bf16[128,2560]{1,0:T(8,128)(2,1)S(1)} %fusion.22, bf16[2560,2048]{1,0:T(8,128)(2,1)} %param.16), kind=kOutput, calls=%fused_computation.29 | convolution fusion | flops 1342439424 | bytes 13238272 | tf_op jit(solution)/shard_map/dot_general | solution.py:77
  135.7 0.2 copy.109
  135.9 0.3 multiply_reduce_fusion
  136.2 0.1 copy.95
  136.3 0.1 copy.96
  136.4 0.3 multiply_multiply_fusion
  136.7 0.5 subtract_convert_fusion
  137.3 0.1 copy.98
  137.4 0.1 copy.97
  137.6 1.1 pad_maximum_fusion
  138.7 67.9 %all-gather.6.cloned.1.call-done = bf16[2048,2,4,128]{3,0,2,1:T(8,128)(2,1)} async-done(((bf16[128,2,4,128]{3,0,2,1:T(8,128)(2,1)}), bf16[2048,2,4,128]{3,0,2,1:T(8,128)(2,1)}) %all-gather.6.cloned.1.call-update) | async-done | bytes 4194320 | tf_op jit(solution)/shard_map/all_gather | solution.py:139
  206.6 29.5 %while.14 = (s32[]{:T(128)}, f32[128,4,4]{0,2,1:T(4,128)S(1)}, f32[128,4,4,128]{0,3,2,1:T(8,128)S(1)}, s32[1,4]{1,0:T(1,128)S(1)}, s32[2]{0:T(128)S(1)}, /*index...) while((s32[]{:T(128)}, f32[128,4,4]{0,2,1:T(4,128)S(1)}, ...), condition=%wide.region_12.13_spmd.clone, body=%wide.region_9.12_spmd.clone.sunk | while | flops 1087389824 | bytes 28237536 | solution.py:170
  206.6 0.7 dynamic_slice.21
  207.2 0.7 iota_add_fusion.6
  207.9 0.1 select_reduce_fusion.5
  208.0 0.7 broadcast_compare_fusion.2
  208.7 0.9 and_and_fusion.2
  209.6 1.7 dynamic-slice_bitcast_fusion.2
  211.4 4.9 %fusion.54 = (f32[128,4,4]{0,2,1:T(4,128)S(1)}, f32[4,1024,128,4]{2,1,3,0:T(8,128)}) fusion(pred[128,1024]{0,1:T(8,128)(4,1)S(1)} %and_and_fusion.2, bf16[128,4,4,128]{3,0,2,1:T(8,128)(2,1)S(1)} %copy-done, bf16[1024,2,4,128]{3,0,2,1:T(8,128)(2,1)S(1)} %dynamic-slice_bitcast_fusion.2), kind=kOutput, calls=%fused_computation.3.clone.1 | convolution fusion | flops 543160320 | bytes 10100736 | tf_op jit(solution)/shard_map/while/body/eval_jaxpr/tkgd,skd->tkgs/dot_general | solution.py:157
  216.3 4.9 %fusion.55 = f32[128,4,4,128]{0,3,2,1:T(8,128)S(1)} fusion(f32[4,1024,128,4]{2,1,3,0:T(8,128)} %get-tuple-element.280, pred[128,1024]{0,1:T(8,128)(4,1)S(1)} %and_and_fusion.2, bf16[1024,2,4,128]{3,0,2,1:T(8,128)(2,1)S(1)} %dynamic-slice_bitcast_fusion.2, f32[128,4,4,128]{0,3,2,1:T(8,128)S(1)} %get-tuple-element.295, pred[]{:T(512)S(6)} %compare.3), kind=kOutput, calls=%fused_computation.10.clone.1 | convolution fusion | flops 543686656 | bytes 11665409 | tf_op jit(solution)/shard_map/while/body/eval_jaxpr/tkgs,skd->tkgd/dot_general | solution.py:162
  221.3 0.7 dynamic_slice.21
  222.0 0.7 iota_add_fusion.6
  222.7 0.1 select_reduce_fusion.5
  222.8 0.7 broadcast_compare_fusion.2
  223.5 0.9 and_and_fusion.2
  224.4 1.7 dynamic-slice_bitcast_fusion.2
  226.1 4.9 %fusion.54 = (f32[128,4,4]{0,2,1:T(4,128)S(1)}, f32[4,1024,128,4]{2,1,3,0:T(8,128)}) fusion(pred[128,1024]{0,1:T(8,128)(4,1)S(1)} %and_and_fusion.2, bf16[128,4,4,128]{3,0,2,1:T(8,128)(2,1)S(1)} %copy-done, bf16[1024,2,4,128]{3,0,2,1:T(8,128)(2,1)S(1)} %dynamic-slice_bitcast_fusion.2), kind=kOutput, calls=%fused_computation.3.clone.1 | convolution fusion | flops 543160320 | bytes 10100736 | tf_op jit(solution)/shard_map/while/body/eval_jaxpr/tkgd,skd->tkgs/dot_general | solution.py:157
  231.1 4.9 %fusion.55 = f32[128,4,4,128]{0,3,2,1:T(8,128)S(1)} fusion(f32[4,1024,128,4]{2,1,3,0:T(8,128)} %get-tuple-element.280, pred[128,1024]{0,1:T(8,128)(4,1)S(1)} %and_and_fusion.2, bf16[1024,2,4,128]{3,0,2,1:T(8,128)(2,1)S(1)} %dynamic-slice_bitcast_fusion.2, f32[128,4,4,128]{0,3,2,1:T(8,128)S(1)} %get-tuple-element.295, pred[]{:T(512)S(6)} %compare.3), kind=kOutput, calls=%fused_computation.10.clone.1 | convolution fusion | flops 543686656 | bytes 11665409 | tf_op jit(solution)/shard_map/while/body/eval_jaxpr/tkgs,skd->tkgd/dot_general | solution.py:162
  236.0 0.1 divide_convert_fusion
  236.2 1.0 copy.105
  (31 shorter events, 0.3 us)
Async XLA Ops:
  6.5 64.9 %all-gather.4.cloned.1.call-start = ((), (), s32[]{:S(2)}) async-start(), calls=%async_computation | async-start | bytes 2088960 | tf_op jit(solution)/shard_map/all_gather | solution.py:85
  7.3 120.1 %all-gather.8.cloned.1.call-start = ((), (), s32[]{:S(2)}) async-start(), calls=%async_computation.2 | async-start | bytes 1114112 | tf_op jit(solution)/shard_map/all_gather | solution.py:86
  8.0 198.5 %all-gather.6.cloned.1.call-start = ((), (), s32[]{:S(2)}) async-start(), calls=%async_computation.1 | async-start | bytes 4456448 | tf_op jit(solution)/shard_map/all_gather | solution.py:139
  50.3 3.5 %copy-start.2 = (bf16[128]{0:T(256)(128)(2,1)S(1)}, bf16[128]{0:T(256)(128)(2,1)}, u32[]{:S(2)}) copy-start(bf16[128]{0:T(256)(128)(2,1)} %param.19) | copy-start | bytes 772
  54.7 24.7 %copy-start.1 = (s32[4]{0:T(128)S(1)}, s32[4]{0:T(128)}, u32[]{:S(2)}) copy-start(s32[4]{0:T(128)} %param.23) | copy-start | bytes 52
  54.7 24.9 %copy-start.3 = (bf16[128]{0:T(256)(128)(2,1)S(1)}, bf16[128]{0:T(256)(128)(2,1)}, u32[]{:S(2)}) copy-start(bf16[128]{0:T(256)(128)(2,1)} %param.18) | copy-start | bytes 772
  206.6 4.8 %copy-start = (bf16[128,4,4,128]{3,0,2,1:T(8,128)(2,1)S(1)}, bf16[128,4,4,128]{3,0,2,1:T(8,128)(2,1)}, u32[]{:S(2)}) copy-start(bf16[128,4,4,128]{3,0,2,1:T(8,128)(2,1)} %get-tuple-element.313) | copy-start | bytes 1572868 | tf_op jit(solution)/shard_map/while
  221.3 4.8 %copy-start = (bf16[128,4,4,128]{3,0,2,1:T(8,128)(2,1)S(1)}, bf16[128,4,4,128]{3,0,2,1:T(8,128)(2,1)}, u32[]{:S(2)}) copy-start(bf16[128,4,4,128]{3,0,2,1:T(8,128)(2,1)} %get-tuple-element.313) | copy-start | bytes 1572868 | tf_op jit(solution)/shard_map/while
Sparse Core Ops, SparseCore 0:
  10.2 61.1 all-gather.3
  74.1 53.1 all-gather.7
  130.1 76.3 all-gather.5
where the time goes:
time: 247 us; the launch traced here: 244 us
  waiting for transfers between devices  134 us (54%)
  blocking collectives  39.5 us (16%)
  matrix products  34.5 us (14%)
  other arithmetic  15.3 us (6%)
  between operations  13.4 us (5%)
  local copies, waits for them, and re-layouts  7.03 us (3%)
    all_gather x1, waiting for transfers between devices, on_device(): segment = lax.all_gather(key_value, 'req', axis=0, tiled=True)  67.9 us
    all_gather x1, waiting for transfers between devices, on_device(): lax.all_gather(query_up_maps, 'req', axis=0, tiled=True)  47.7 us
    all_gather x1, blocking collectives, on_device(): lax.all_gather(key_value_up_maps, 'req', axis=0, tiled=True)  35.8 us
    all_gather x1, waiting for transfers between devices, on_device(): lax.all_gather(adapter_down_maps, 'req', axis=0, tiled=True)  16.7 us
    dot_general x2, matrix products, key_step(): jnp.einsum('tkgs,skd->tkgd', weights.astype(jnp.bfloat16), key_block[:, 1...  9.88 us
    dot_general x2, matrix products, key_step(): jnp.einsum('tkgd,skd->tkgs', query_every_token, key_block[:, 0], preferre...  9.85 us
    dot_general x1, matrix products, on_device(): jnp.dot(normed, query_weight, preferred_element_type=jnp.float32)  5.51 us
  transfers between devices with their start and end apart: 3, of which 3 were waited for; matrix products, arithmetic and copies ran while one was open for 11% of the time, Pallas kernels for 0%

commit v1 on v0

v1 whole, which is shorter than its diff:
```python
import functools
import math

import jax
import jax.numpy as jnp
import numpy as np
from jax import lax
from jax.experimental import pallas as pl
from jax.experimental.pallas import tpu as pltpu
from jax.sharding import PartitionSpec as P

SHORT_LEN = 64
PLANE = 4
EPSILON = 1e-06
THETA = 1000000.0
ADAPTER_SCALE = 2.0
MASKED = -1e30
MESH = pl.DeviceIdType.MESH


def nt_dot(left, right):
    return lax.dot_general(
        left, right, (((1,), (1,)), ((), ())), preferred_element_type=jnp.float32
    )


def fused_kernel(
    cfg,
    lengths_ref,
    prompt_adapter_ref,
    place_ref,
    tokens_ref,
    gain_ref,
    qgain_ref,
    kgain_ref,
    freq_ref,
    down_ref,
    upq_ref,
    upkv_ref,
    wq_hbm,
    wkv_hbm,
    out_ref,
    wq,
    wkv,
    xn,
    xown,
    slab,
    part1,
    stage2,
    maps,
    dmaps,
    lowp,
    lowr,
    plain_q,
    plain_kv,
    qbuf,
    kvb,
    acc,
    accl,
    cos_t,
    sin_t,
    wq_sem,
    wkv_sem,
    s1_sem,
    r1_sem,
    s2_sem,
    r2_sem,
    sl_sem,
    rl_sem,
    zs_sem,
    zr_sem,
    ps_sem,
    pr_sem,
):
    n, tpn, rows, units = cfg["n"], cfg["tpn"], cfg["rows"], cfg["units"]
    rank, lw, dseg, piece, pieces = (
        cfg["rank"],
        cfg["lw"],
        cfg["dseg"],
        cfg["piece"],
        cfg["pieces"],
    )
    nkv, group, hw = cfg["nkv"], cfg["group"], cfg["hw"]
    kvw, gw = nkv * hw, group * hw
    planes, back = n // PLANE, n // 2 // PLANE
    me = lax.axis_index("req")
    tp = lax.axis_index("tp")
    hi = lax.div(me, PLANE)
    lo = lax.rem(me, PLANE)

    def q_copy(c):
        return pltpu.make_async_copy(
            wq_hbm.at[:, pl.ds(pl.multiple_of(c * gw, 128), gw)], wq.at[c], wq_sem.at[c]
        )

    def kv_copy(c):
        return pltpu.make_async_copy(wkv_hbm.at[c], wkv.at[c], wkv_sem.at[c])

    for c in range(2):
        kv_copy(c).start()
    for c in range(nkv):
        q_copy(c).start()

    barrier = pltpu.get_barrier_semaphore()

    def greet(k, carry):
        pl.semaphore_signal(
            barrier, inc=1, device_id=(lax.rem(me + k, n), tp), device_id_type=MESH
        )
        return carry

    lax.fori_loop(1, n, greet, 0)
    for k in range(1, tpn):
        pl.semaphore_signal(
            barrier, inc=1, device_id=(me, lax.rem(tp + k, tpn)), device_id_type=MESH
        )

    if dseg > lw:
        slab[...] = jnp.zeros_like(slab)
    for r in range(3):
        slab[:, r * dseg : r * dseg + lw] = down_ref[0, r * rank : (r + 1) * rank, :]
    base = 3 * dseg
    slab[:, base : base + nkv * gw] = upq_ref[0]
    for c in range(2):
        at = base + nkv * gw + c * kvw
        slab[:, at : at + kvw] = upkv_ref[0, c]
    used = base + nkv * gw + 2 * kvw
    if pieces * piece > used:
        slab[:, used:] = jnp.zeros((rank, pieces * piece - used), slab.dtype)

    pl.semaphore_wait(barrier, n - 1 + tpn - 1)

    def lanes(index):
        return pl.ds(pl.multiple_of(index * piece, 128), piece)

    def first_copy(dest, source):
        return pltpu.make_async_remote_copy(
            src_ref=slab.at[:, lanes(dest)],
            dst_ref=part1.at[source],
            send_sem=s1_sem.at[dest],
            recv_sem=r1_sem.at[source],
            device_id=(dest, tp),
            device_id_type=MESH,
        )

    def first_send(k, carry):
        dest = lax.rem(me + k, n)

        @pl.when(dest < pieces)
        def _():
            first_copy(dest, me).start()

        return carry

    lax.fori_loop(1, n, first_send, 0)

    values = tokens_ref[...].astype(jnp.float32)
    inverse = lax.rsqrt(jnp.mean(values * values, axis=-1, keepdims=True) + EPSILON)
    xn[...] = (values * inverse * gain_ref[...].astype(jnp.float32)).astype(jnp.bfloat16)
    if dseg > lw:
        xown[...] = jnp.zeros_like(xown)
    for k in range(tpn):

        @pl.when(tp == k)
        def _():
            xown[:, :lw] = xn[:, k * lw : (k + 1) * lw]

    def kv_product(c, carry):
        kv_copy(c).wait()
        plain_kv[c] = jnp.dot(xn[...], wkv[c], preferred_element_type=jnp.float32)
        return carry

    lax.fori_loop(0, 2, kv_product, 0)

    count = lengths_ref.shape[0]
    ends = []
    running = jnp.int32(0)
    for j in range(count):
        running = running + lengths_ref[j]
        ends.append(running)

    def slot_of(position):
        prompt = jnp.int32(0)
        for j in range(count - 1):
            prompt = prompt + (ends[j] <= position).astype(jnp.int32)
        return place_ref[prompt_adapter_ref[prompt]]

    def second_copy(dest, source):
        return pltpu.make_async_remote_copy(
            src_ref=stage2.at[dest],
            dst_ref=maps.at[:, :, lanes(source)],
            send_sem=s2_sem.at[dest],
            recv_sem=r2_sem.at[source],
            device_id=(dest, tp),
            device_id_type=MESH,
        )

    @pl.when(me < pieces)
    def _():
        part1[me] = slab[:, lanes(me)]

        def first_wait(k, carry):
            source = lax.rem(me + k, n)
            first_copy(me, source).wait_recv()
            return carry

        lax.fori_loop(1, n, first_wait, 0)

        def second_send(k, carry):
            dest = lax.rem(me + k, n)
            for u in range(units):
                stage2[dest, u] = part1[slot_of((dest * units + u) * SHORT_LEN)]
            second_copy(dest, me).start()
            return carry

        lax.fori_loop(1, n, second_send, 0)
        for u in range(units):
            maps[u, :, lanes(me)] = part1[slot_of((me * units + u) * SHORT_LEN)]

    def q_product(c, carry):
        q_copy(c).wait()
        plain_q[c] = jnp.dot(xn[...], wq[c], preferred_element_type=jnp.float32)
        return carry

    lax.fori_loop(0, nkv, q_product, 0)

    row_pos = me * rows + lax.broadcasted_iota(jnp.int32, (rows, hw), 0)
    row_start = jnp.zeros((rows, hw), jnp.int32)
    for j in range(count):
        row_start = row_start + jnp.where(ends[j] <= row_pos, lengths_ref[j], 0)
    angles = (row_pos - row_start).astype(jnp.float32) * freq_ref[...]
    sine = jnp.sin(angles)
    cos_t[...] = jnp.cos(angles)
    lane = lax.broadcasted_iota(jnp.int32, (rows, hw), 1)
    sin_t[...] = jnp.where(lane < hw // 2, -sine, sine)
    dmaps[...] = jnp.zeros_like(dmaps)
    acc[...] = jnp.zeros_like(acc)
    accl[...] = jnp.zeros_like(accl)

    def second_wait(k, carry):
        source = lax.rem(me + k, n)

        @pl.when(source < pieces)
        def _():
            second_copy(me, source).wait_recv()

        return carry

    lax.fori_loop(1, n, second_wait, 0)

    for u in range(units):
        for r in range(3):
            dmaps[u, r * rank : (r + 1) * rank, :] = maps[u, :, r * dseg : (r + 1) * dseg]
        rows_u = slice(u * SHORT_LEN, (u + 1) * SHORT_LEN)
        lowp[rows_u, :] = nt_dot(xown[rows_u, :], dmaps[u])

    def low_copy(k, source):
        return pltpu.make_async_remote_copy(
            src_ref=lowp,
            dst_ref=lowr.at[source],
            send_sem=sl_sem.at[k],
            recv_sem=rl_sem.at[source],
            device_id=(me, lax.rem(tp + k, tpn)),
            device_id_type=MESH,
        )

    for k in range(1, tpn):
        low_copy(k, tp).start()
    low = lowp[...]
    for k in range(1, tpn):
        source = lax.rem(tp + k, tpn)
        low_copy(tpn - k, source).wait_recv()
        low = low + lowr[source]
    low = low.astype(jnp.bfloat16)

    def increment(part, start, width):
        return [
            jnp.dot(
                low[u * SHORT_LEN : (u + 1) * SHORT_LEN, part * rank : (part + 1) * rank],
                maps[u, :, pl.ds(start, width)],
                preferred_element_type=jnp.float32,
            )
            for u in range(units)
        ]

    def head(values, gain):
        inverse = lax.rsqrt(jnp.mean(values * values, axis=-1, keepdims=True) + EPSILON)
        values = values * inverse * gain
        return (values * cos_t[...] + pltpu.roll(values, hw // 2, 1) * sin_t[...]).astype(
            jnp.bfloat16
        )

    kgain = kgain_ref[...].astype(jnp.float32)
    qgain = qgain_ref[...].astype(jnp.float32)
    k_at = base + nkv * gw
    k_raw = plain_kv[0] + ADAPTER_SCALE * jnp.concatenate(increment(1, k_at, kvw), 0)
    v_raw = plain_kv[1] + ADAPTER_SCALE * jnp.concatenate(increment(2, k_at + kvw, kvw), 0)
    for k in range(nkv):
        kvb[0, lo, 0, :, k * hw : (k + 1) * hw] = head(k_raw[:, k * hw : (k + 1) * hw], kgain)
    kvb[0, lo, 1] = v_raw.astype(jnp.bfloat16)

    xn_lo = lo + 1 - 2 * lax.rem(lo, 2)
    yn_lo = lax.rem(lo + 2, PLANE)
    dn_lo = PLANE - 1 - lo

    def need(s, source, dest):
        if s == 0:
            return source < dest
        if s == back:
            return source > dest
        return source >= 0

    def z_copy(s):
        return pltpu.make_async_remote_copy(
            src_ref=kvb.at[s, lo],
            dst_ref=kvb.at[s + 1, lo],
            send_sem=zs_sem.at[s],
            recv_sem=zr_sem.at[s + 1],
            device_id=(lax.rem(me + PLANE, n), tp),
            device_id_type=MESH,
        )

    def p_copy(kind, s, block, half, dest):
        return pltpu.make_async_remote_copy(
            src_ref=kvb.at[s, block, half],
            dst_ref=kvb.at[s, block, half],
            send_sem=ps_sem.at[kind, s],
            recv_sem=pr_sem.at[kind, s],
            device_id=(hi * PLANE + dest, tp),
            device_id_type=MESH,
        )

    def plan(s, sender, x_of, y_of, d_of):
        return (
            (0, sender, 0, x_of, need(s, sender, x_of)),
            (1, sender, 1, x_of, need(s, sender, x_of) | need(s, sender, d_of)),
            (2, sender, 0, y_of, need(s, sender, y_of) | need(s, sender, d_of)),
            (3, sender, 1, y_of, need(s, sender, y_of)),
        )

    def relays(s):
        return (
            (4, yn_lo, 0, xn_lo, need(s, yn_lo, xn_lo)),
            (5, xn_lo, 1, yn_lo, need(s, xn_lo, yn_lo)),
        )

    def launch(s):
        if s < back:

            @pl.when((hi >= s) & (hi + 1 < planes))
            def _():
                z_copy(s).start()

        for kind, block, half, dest, wanted in plan(s, lo, xn_lo, yn_lo, dn_lo):

            @pl.when((hi >= s) & wanted)
            def _():
                p_copy(kind, s, block, half, dest).start()

    def arrive(s):
        from_x = plan(s, xn_lo, lo, dn_lo, yn_lo)[:2]
        from_y = plan(s, yn_lo, dn_lo, lo, xn_lo)[2:]
        for (kind, block, half, dest, wanted), relay in zip(
            (from_y[0], from_x[1], from_x[0], from_y[1]), relays(s) + (None, None)
        ):

            @pl.when((hi >= s) & wanted)
            def _():
                p_copy(kind, s, block, half, dest).wait_recv()

            if relay is not None:
                r_kind, r_block, r_half, r_dest, r_wanted = relay

                @pl.when((hi >= s) & r_wanted)
                def _():
                    p_copy(r_kind, s, r_block, r_half, r_dest).start()

    def diagonal(s):
        @pl.when((hi >= s) & need(s, dn_lo, lo))
        def _():
            p_copy(4, s, dn_lo, 0, lo).wait_recv()
            p_copy(5, s, dn_lo, 1, lo).wait_recv()

    factor = math.log2(math.e) / math.sqrt(hw)

    def attend(s, block, wanted):
        @pl.when((hi >= s) & wanted)
        def _():
            key_pos = ((hi - s) * PLANE + block) * rows + lax.broadcasted_iota(
                jnp.int32, (rows, rows), 1
            )
            query_pos = me * rows + lax.broadcasted_iota(jnp.int32, (rows, rows), 0)
            first = jnp.zeros((rows, rows), jnp.int32)
            for j in range(count):
                first = first + jnp.where(ends[j] <= query_pos, lengths_ref[j], 0)
            bias = jnp.where((key_pos >= first) & (key_pos <= query_pos), 0.0, MASKED)
            bias = jnp.concatenate([bias] * group, 0)
            for k in range(nkv):
                cols = slice(k * hw, (k + 1) * hw)
                weights = jnp.exp2(nt_dot(qbuf[k], kvb[s, block, 0, :, cols]) * factor + bias)
                accl[k] += weights
                acc[k] += jnp.dot(
                    weights.astype(jnp.bfloat16),
                    kvb[s, block, 1, :, cols],
                    preferred_element_type=jnp.float32,
                )

    launch(0)

    def q_final(c, carry):
        start = pl.multiple_of(base + c * gw, 128)
        raw = plain_q[c] + ADAPTER_SCALE * jnp.concatenate(increment(0, start, gw), 0)
        for g in range(group):
            qbuf[c, g * rows : (g + 1) * rows, :] = head(raw[:, g * hw : (g + 1) * hw], qgain)
        return carry

    lax.fori_loop(0, nkv, q_final, 0)

    for s in range(back + 1):
        if s < back:

            @pl.when(hi >= s + 1)
            def _():
                z_copy(s).wait_recv()

            launch(s + 1)
        arrive(s)
        attend(s, lo, lo >= 0)
        attend(s, xn_lo, need(s, xn_lo, lo))
        attend(s, yn_lo, need(s, yn_lo, lo))
        if s >= 1:
            diagonal(s - 1)
            attend(s - 1, dn_lo, need(s - 1, dn_lo, lo))
    diagonal(back)
    attend(back, dn_lo, need(back, dn_lo, lo))

    for k in range(nkv):
        total = jnp.sum(accl[k], axis=-1, keepdims=True)
        result = (acc[k] / total).astype(out_ref.dtype)
        for g in range(group):
            at = (k * group + g) * hw
            out_ref[:, at : at + hw] = result[g * rows : (g + 1) * rows, :]

    def drain(k, carry):
        dest = lax.rem(me + k, n)

        @pl.when(dest < pieces)
        def _():
            first_copy(dest, me).wait_send()

        @pl.when(me < pieces)
        def _():
            second_copy(dest, me).wait_send()

        return carry

    lax.fori_loop(1, n, drain, 0)
    for k in range(1, tpn):
        low_copy(k, tp).wait_send()
    for s in range(back + 1):
        if s < back:

            @pl.when((hi >= s) & (hi + 1 < planes))
            def _():
                z_copy(s).wait_send()

        for kind, block, half, dest, wanted in (
            plan(s, lo, xn_lo, yn_lo, dn_lo) + relays(s)
        ):

            @pl.when((hi >= s) & wanted)
            def _():
                p_copy(kind, s, block, half, dest).wait_send()


def on_device(
    n,
    tpn,
    tokens,
    input_norm_gain,
    query_weight,
    key_value_weight,
    query_head_gain,
    key_head_gain,
    adapter_down_maps,
    query_up_maps,
    key_value_up_maps,
    packed_lengths,
    adapter_per_prompt,
    adapter_place,
):
    rows, width = tokens.shape
    hw = query_head_gain.shape[0]
    nkv = key_value_weight.shape[2] // hw
    group = query_weight.shape[1] // hw // nkv
    rank, lw = query_up_maps.shape[1], adapter_down_maps.shape[2]
    units = rows // SHORT_LEN
    dseg = -(-lw // 128) * 128
    kvw, gw = nkv * hw, group * hw
    used = 3 * dseg + nkv * gw + 2 * kvw
    tiles = used // 128
    piece = -(-tiles // n) * 128
    pieces = -(-used // piece)
    back = n // 2 // PLANE
    cfg = dict(
        n=n,
        tpn=tpn,
        rows=rows,
        units=units,
        rank=rank,
        lw=lw,
        dseg=dseg,
        piece=piece,
        pieces=pieces,
        nkv=nkv,
        group=group,
        hw=hw,
    )
    powers = np.arange(hw // 2, dtype=np.float64) * (2.0 / hw)
    frequency = (THETA ** (-powers)).astype(np.float32)
    frequency = jnp.asarray(np.concatenate([frequency, frequency])[None, :])
    smem = pl.BlockSpec(memory_space=pltpu.SMEM)
    vmem = pl.BlockSpec(memory_space=pltpu.VMEM)
    hbm = pl.BlockSpec(memory_space=pl.ANY)
    bf, f32 = jnp.bfloat16, jnp.float32
    dma = pltpu.SemaphoreType.DMA
    call = pl.pallas_call(
        functools.partial(fused_kernel, cfg),
        out_shape=jax.ShapeDtypeStruct((rows, nkv * gw), bf),
        in_specs=[smem] * 3 + [vmem] * 8 + [hbm] * 2,
        out_specs=vmem,
        scratch_shapes=[
            pltpu.VMEM((nkv, width, gw), bf),
            pltpu.VMEM((2, width, kvw), bf),
            pltpu.VMEM((rows, width), bf),
            pltpu.VMEM((rows, dseg), bf),
            pltpu.VMEM((rank, pieces * piece), bf),
            pltpu.VMEM((n, rank, piece), bf),
            pltpu.VMEM((n, units, rank, piece), bf),
            pltpu.VMEM((units, rank, pieces * piece), bf),
            pltpu.VMEM((units, 128, dseg), bf),
            pltpu.VMEM((rows, 128), f32),
            pltpu.VMEM((tpn, rows, 128), f32),
            pltpu.VMEM((nkv, rows, gw), f32),
            pltpu.VMEM((2, rows, kvw), f32),
            pltpu.VMEM((nkv, group * rows, hw), bf),
            pltpu.VMEM((back + 1, PLANE, 2, rows, kvw), bf),
            pltpu.VMEM((nkv, group * rows, hw), f32),
            pltpu.VMEM((nkv, group * rows, rows), f32),
            pltpu.VMEM((rows, hw), f32),
            pltpu.VMEM((rows, hw), f32),
            dma((nkv,)),
            dma((2,)),
            dma((n,)),
            dma((n,)),
            dma((n,)),
            dma((n,)),
            dma((tpn,)),
            dma((tpn,)),
            dma((back + 1,)),
            dma((back + 1,)),
            dma((6, back + 1)),
            dma((6, back + 1)),
        ],
        compiler_params=pltpu.CompilerParams(
            collective_id=0, has_side_effects=True, vmem_limit_bytes=50 << 20
        ),
    )
    return call(
        packed_lengths,
        adapter_per_prompt,
        adapter_place,
        tokens,
        input_norm_gain.reshape(1, -1),
        query_head_gain.reshape(1, -1),
        key_head_gain.reshape(1, -1),
        frequency,
        adapter_down_maps,
        query_up_maps,
        key_value_up_maps,
        query_weight,
        key_value_weight,
    )


def solution(mesh):
    in_specs = (
        P("req", None),
        P(),
        P(None, "tp"),
        P(None, None, "tp"),
        P(),
        P(),
        P("req", None, "tp"),
        P("req", None, "tp"),
        P("req", None, None, "tp"),
        P(),
        P(),
        P(),
    )
    body = functools.partial(on_device, mesh.shape["req"], mesh.shape["tp"])
    return jax.shard_map(
        body, mesh=mesh, in_specs=in_specs, out_specs=P("req", "tp"), check_vma=False
    )
```

time: 247 us -> 64.3 us (0.26); the launches traced: 244 us -> 63.9 us
  waiting for transfers between devices: 134 us -> 0 us
  Pallas kernels: 0 us -> 54.8 us
  blocking collectives: 39.5 us -> 0 us
  matrix products: 34.5 us -> 0 us
  other arithmetic: 15.3 us -> 0 us
  between operations: 13.4 us -> 0.02 us
    all_gather x3 -> x0, waiting for transfers between devices: 132 us -> none  [the longest x1 67.9 us: on_device(): segment = lax.all_gather(key_value, 'req', axis=0, tiled=True)]
    pallas_call x0 -> x1, Pallas kernels: none -> 54.8 us  [on_device(): call(packed_lengths, adapter_per_prompt, adapter_place, tokens, input_nor...]
    all_gather x1 -> x0, blocking collectives: 35.8 us -> none  [on_device(): lax.all_gather(key_value_up_maps, 'req', axis=0, tiled=True)]
    dot_general x12 -> x0, matrix products: 34.5 us -> none  [the longest x2 9.88 us: key_step(): jnp.einsum('tkgs,skd->tkgd', weights.astype(jnp.bfloat16), key_block[:, 1...]
    unnamed x7 -> x21, local copies, waits for them, and re-layouts: 0.21 us -> 8.31 us
    psum x1 -> x0, blocking collectives: 3.69 us -> none  [on_device(): reduced_rank = lax.psum(partial_sum, 'tp').astype(jnp.bfloat16)]
    squeeze x4 -> x0, local copies, waits for them, and re-layouts: 3.68 us -> none  [the longest x2 3.5 us: on_device(): result = lax.scan(key_step, start_sums, (blocks, block_first))[0]]
    reduce_sum x7 -> x0, other arithmetic: 3.45 us -> none  [the longest x3 1.79 us: normalize(): jnp.mean(values * values, axis=-1, keepdims=True) + epsilon]
  transfers between devices with their start and end apart: 3 -> 0, of which waited for: 3 -> 0; matrix products, arithmetic and copies ran while one was open for 11% -> 0% of each run, Pallas kernels for 0% -> 0%
where the time goes in v1:
time: 64.3 us; the launch traced here: 63.9 us
  Pallas kernels  54.8 us (85%)
  local copies, waits for them, and re-layouts  9 us (14%)
    pallas_call x1, Pallas kernels, on_device(): call(packed_lengths, adapter_per_prompt, adapter_place, tokens, input_nor...  54.8 us
    unnamed x21, local copies, waits for them, and re-layouts  8.31 us

profile of v1, /device:TPU:16, one launch (start us, length us, event | category | flops | bytes accessed | tf_op | source)
XLA Modules:
  0.0 63.9 jit_solution(18371181823226263697)
XLA Ops:
  0.0 0.7 %reshape.9.gain_ref = bf16[1,2560]{1,0:T(2,128)(2,1)S(1)} reshape(bf16[2560]{0:T(1024)(128)(2,1)} %param.14) | data formatting | bytes 10240 | tf_op jit(solution)/shard_map/reshape | solution.py:574
  0.7 0.0 copy-start
  0.7 1.1 %copy-done = bf16[128,2560]{1,0:T(8,128)(2,1)S(1)} copy-done((bf16[128,2560]{1,0:T(8,128)(2,1)S(1)}, bf16[128,2560]{1,0:T(8,128)(2,1)}, u32[]{:S(2)}) %copy-start) | copy-done | bytes 655384
  1.8 0.0 copy-start.1
  1.8 0.9 %copy-done.1 = bf16[1,48,1280]{2,1,0:T(8,128)(2,1)S(1)} copy-done((bf16[1,48,1280]{2,1,0:T(8,128)(2,1)S(1)}, bf16[1,48,1280]{2,1,0:T(8,128)(2,1)}, u32[]{:S(2)}) %copy-start.1) | copy-done | bytes 122904
  2.7 0.0 copy-start.2
  2.7 0.8 %copy-done.2 = bf16[1,16,2048]{2,1,0:T(8,128)(2,1)S(1)} copy-done((bf16[1,16,2048]{2,1,0:T(8,128)(2,1)S(1)}, bf16[1,16,2048]{2,1,0:T(8,128)(2,1)}, u32[]{:S(2)}) %copy-start.2) | copy-done | bytes 65560
  3.5 0.0 copy-start.3
  3.5 0.8 %copy-done.3 = bf16[1,2,16,512]{3,2,1,0:T(8,128)(2,1)S(1)} copy-done((bf16[1,2,16,512]{3,2,1,0:T(8,128)(2,1)S(1)}, bf16[1,2,16,512]{3,2,1,0:T(8,128)(2,1)}, u32[]{:S(2)}) %copy-start.3) | copy-done | bytes 32792
  4.3 0.0 copy-start.4
  4.3 0.7 %copy-done.4 = s32[4]{0:T(128)S(1)} copy-done((s32[4]{0:T(128)S(1)}, s32[4]{0:T(128)}, u32[]{:S(2)}) %copy-start.4) | copy-done | bytes 40
  4.9 0.0 copy-start.5
  4.9 0.7 %copy-done.5 = s32[4]{0:T(128)S(1)} copy-done((s32[4]{0:T(128)S(1)}, s32[4]{0:T(128)}, u32[]{:S(2)}) %copy-start.5) | copy-done | bytes 40
  5.6 0.0 copy-start.6
  5.6 0.7 %copy-done.6 = s32[16]{0:T(128)S(1)} copy-done((s32[16]{0:T(128)S(1)}, s32[16]{0:T(128)}, u32[]{:S(2)}) %copy-start.6) | copy-done | bytes 88
  6.3 0.0 copy-start.7
  6.3 0.7 %copy-done.7 = bf16[128]{0:T(256)(128)(2,1)S(1)} copy-done((bf16[128]{0:T(256)(128)(2,1)S(1)}, bf16[128]{0:T(256)(128)(2,1)}, u32[]{:S(2)}) %copy-start.7) | copy-done | bytes 280
  6.9 0.0 copy-start.8
  6.9 0.7 %copy-done.8 = bf16[128]{0:T(256)(128)(2,1)S(1)} copy-done((bf16[128]{0:T(256)(128)(2,1)S(1)}, bf16[128]{0:T(256)(128)(2,1)}, u32[]{:S(2)}) %copy-start.8) | copy-done | bytes 280
  7.6 0.0 copy-start.9
  7.6 0.7 %copy-done.9 = f32[1,128]{1,0:T(1,128)S(1)} copy-done((f32[1,128]{1,0:T(1,128)S(1)}, f32[1,128]{1,0:T(1,128)}, u32[]{:S(2)}) %copy-start.9) | copy-done | bytes 536
  8.2 54.8 %shard_map.127 = bf16[128,2048]{1,0:T(8,128)(2,1)S(1)} custom-call(s32[4]{0:T(128)S(1)} %copy-done.4, s32[4]{0:T(128)S(1)} %copy-done.5, s32[16]{0:T(128)S(1)} %copy-done.6, bf16[128,2560]{1,0:T(8,128)(2,1)S(1)} %copy-done, bf16[1,2560]{1,0:T(2,128)(2,1)S(1)} %reshape.9.gain_ref, bf16[1,128]{1,0:T(2,128)(2,1)S(1)} %bitcast.2, bf16[1,128]{1,0:T(2,128)(2,1)S(1)} %bitcast.3, ...), custom_call_target="tpu_custom_call" | custom-call | tf_op jit(solution)/shard_map/pallas_call | solution.py:569
  63.1 0.8 %copy.15 = bf16[128,2048]{1,0:T(8,128)(2,1)} copy(bf16[128,2048]{1,0:T(8,128)(2,1)S(1)} %shard_map.127) | data formatting | bytes 1048576
Async XLA Ops:
  0.7 1.1 %copy-start = (bf16[128,2560]{1,0:T(8,128)(2,1)S(1)}, bf16[128,2560]{1,0:T(8,128)(2,1)}, u32[]{:S(2)}) copy-start(bf16[128,2560]{1,0:T(8,128)(2,1)} %tokens_ref.1) | copy-start | bytes 1966084
  1.8 0.9 %copy-start.1 = (bf16[1,48,1280]{2,1,0:T(8,128)(2,1)S(1)}, bf16[1,48,1280]{2,1,0:T(8,128)(2,1)}, u32[]{:S(2)}) copy-start(bf16[1,48,1280]{2,1,0:T(8,128)(2,1)} %down_ref.1) | copy-start | bytes 368644
  2.7 0.8 %copy-start.2 = (bf16[1,16,2048]{2,1,0:T(8,128)(2,1)S(1)}, bf16[1,16,2048]{2,1,0:T(8,128)(2,1)}, u32[]{:S(2)}) copy-start(bf16[1,16,2048]{2,1,0:T(8,128)(2,1)} %upq_ref.1) | copy-start | bytes 196612
  3.5 0.8 %copy-start.3 = (bf16[1,2,16,512]{3,2,1,0:T(8,128)(2,1)S(1)}, bf16[1,2,16,512]{3,2,1,0:T(8,128)(2,1)}, u32[]{:S(2)}) copy-start(bf16[1,2,16,512]{3,2,1,0:T(8,128)(2,1)} %upkv_ref.1) | copy-start | bytes 98308
  4.3 0.7 %copy-start.4 = (s32[4]{0:T(128)S(1)}, s32[4]{0:T(128)}, u32[]{:S(2)}) copy-start(s32[4]{0:T(128)} %lengths_ref.1) | copy-start | bytes 52
  4.9 0.7 %copy-start.5 = (s32[4]{0:T(128)S(1)}, s32[4]{0:T(128)}, u32[]{:S(2)}) copy-start(s32[4]{0:T(128)} %prompt_adapter_ref.1) | copy-start | bytes 52
  5.6 0.7 %copy-start.6 = (s32[16]{0:T(128)S(1)}, s32[16]{0:T(128)}, u32[]{:S(2)}) copy-start(s32[16]{0:T(128)} %place_ref.1) | copy-start | bytes 196
  6.3 0.7 %copy-start.7 = (bf16[128]{0:T(256)(128)(2,1)S(1)}, bf16[128]{0:T(256)(128)(2,1)}, u32[]{:S(2)}) copy-start(bf16[128]{0:T(256)(128)(2,1)} %param.17) | copy-start | bytes 772
  6.9 0.7 %copy-start.8 = (bf16[128]{0:T(256)(128)(2,1)S(1)}, bf16[128]{0:T(256)(128)(2,1)}, u32[]{:S(2)}) copy-start(bf16[128]{0:T(256)(128)(2,1)} %param.18) | copy-start | bytes 772
  7.6 0.7 %copy-start.9 = (f32[1,128]{1,0:T(1,128)S(1)}, f32[1,128]{1,0:T(1,128)}, u32[]{:S(2)}) copy-start(f32[1,128]{1,0:T(1,128)} %constant.2.clone.freq_ref) | copy-start | bytes 1540

commit v2 on v1

v2 whole, which is shorter than its diff:
```python
import functools
import math

import jax
import jax.numpy as jnp
import numpy as np
from jax import lax
from jax.experimental import pallas as pl
from jax.experimental.pallas import tpu as pltpu
from jax.sharding import PartitionSpec as P

SHORT_LEN = 64
PLANE = 4
EPSILON = 1e-06
THETA = 1000000.0
ADAPTER_SCALE = 2.0
MASKED = -1e30
MESH = pl.DeviceIdType.MESH


def nt_dot(left, right):
    return lax.dot_general(
        left, right, (((1,), (1,)), ((), ())), preferred_element_type=jnp.float32
    )


def fused_kernel(
    cfg,
    lengths_hbm,
    prompt_adapter_hbm,
    place_hbm,
    tokens_hbm,
    gain_hbm,
    qgain_hbm,
    kgain_hbm,
    freq_hbm,
    down_hbm,
    upq_hbm,
    upkv_hbm,
    wq_hbm,
    wkv_hbm,
    out_ref,
    lengths_ref,
    prompt_adapter_ref,
    place_ref,
    tokens_ref,
    gain_ref,
    qgain_ref,
    kgain_ref,
    freq_ref,
    down_ref,
    upq_ref,
    upkv_ref,
    wq,
    wkv,
    xn,
    xown,
    slab_a,
    slab_b,
    part_a,
    part_b,
    stage_a,
    stage_b,
    maps_a,
    maps_b,
    dmaps,
    lowp,
    lowr,
    plain_q,
    plain_k,
    qbuf,
    kb0,
    kb1,
    vb0,
    vb1,
    acc,
    accl,
    accd,
    cos_t,
    sin_t,
    in_sem,
    wq_sem,
    wkv_sem,
    s1_sem,
    r1_sem,
    s2_sem,
    r2_sem,
    sl_sem,
    rl_sem,
    zs_sem,
    zr_sem,
    ps_sem,
    pr_sem,
):
    n, tpn, rows, units = cfg["n"], cfg["tpn"], cfg["rows"], cfg["units"]
    rank, lw, dseg = cfg["rank"], cfg["lw"], cfg["dseg"]
    nkv, group, hw = cfg["nkv"], cfg["group"], cfg["hw"]
    kvw, gw, half_rows = nkv * hw, group * hw, rows // 2
    planes, back = n // PLANE, n // 2 // PLANE
    me = lax.axis_index("req")
    tp = lax.axis_index("tp")
    hi = lax.div(me, PLANE)
    lo = lax.rem(me, PLANE)

    def q_copy(c):
        return pltpu.make_async_copy(
            wq_hbm.at[:, pl.ds(pl.multiple_of(c * gw, 128), gw)], wq.at[c], wq_sem.at[c]
        )

    def kv_copy(c):
        return pltpu.make_async_copy(wkv_hbm.at[c], wkv.at[c], wkv_sem.at[c])

    loads = [
        pltpu.make_async_copy(source, dest, in_sem.at[i])
        for i, (source, dest) in enumerate(
            (
                (down_hbm, down_ref),
                (upkv_hbm, upkv_ref),
                (upq_hbm, upq_ref),
                (tokens_hbm, tokens_ref),
                (gain_hbm, gain_ref),
                (lengths_hbm, lengths_ref),
                (prompt_adapter_hbm, prompt_adapter_ref),
                (place_hbm, place_ref),
                (freq_hbm, freq_ref),
                (qgain_hbm, qgain_ref),
                (kgain_hbm, kgain_ref),
            )
        )
    ]
    for load in loads:
        load.start()
    kv_copy(1).start()
    kv_copy(0).start()
    for c in range(nkv):
        q_copy(c).start()

    barrier = pltpu.get_barrier_semaphore()

    def greet(k, carry):
        pl.semaphore_signal(
            barrier, inc=1, device_id=(lax.rem(me + k, n), tp), device_id_type=MESH
        )
        return carry

    lax.fori_loop(1, n, greet, 0)
    for k in range(1, tpn):
        pl.semaphore_signal(
            barrier, inc=1, device_id=(me, lax.rem(tp + k, tpn)), device_id_type=MESH
        )
    for load in loads[:3]:
        load.wait()

    slab_a[...] = jnp.zeros_like(slab_a)
    slab_b[...] = jnp.zeros_like(slab_b)
    slab_b[:, :lw] = down_ref[0, :rank, :]
    slab_a[:, :lw] = down_ref[0, rank : 2 * rank, :]
    slab_a[:, dseg : dseg + lw] = down_ref[0, 2 * rank : 3 * rank, :]
    k_at, q_at = 2 * dseg, dseg
    v_at = q_at + nkv * gw
    slab_a[:, k_at : k_at + kvw] = upkv_ref[0, 0]
    slab_b[:, q_at : q_at + nkv * gw] = upq_ref[0]
    slab_b[:, v_at : v_at + kvw] = upkv_ref[0, 1]

    pl.semaphore_wait(barrier, n - 1 + tpn - 1)

    groups = (
        (slab_a, part_a, stage_a, maps_a, cfg["piece_a"], cfg["pieces_a"]),
        (slab_b, part_b, stage_b, maps_b, cfg["piece_b"], cfg["pieces_b"]),
    )

    def lanes(index, piece):
        return pl.ds(pl.multiple_of(index * piece, 128), piece)

    def first_copy(x, dest, source):
        slab, part, _, _, piece, _ = groups[x]
        return pltpu.make_async_remote_copy(
            src_ref=slab.at[:, lanes(dest, piece)],
            dst_ref=part.at[source],
            send_sem=s1_sem.at[x, dest],
            recv_sem=r1_sem.at[x, source],
            device_id=(dest, tp),
            device_id_type=MESH,
        )

    def first_phase(x):
        def first_send(k, carry):
            dest = lax.rem(me + k, n)

            @pl.when(dest < groups[x][5])
            def _():
                first_copy(x, dest, me).start()

            return carry

        lax.fori_loop(1, n, first_send, 0)

    first_phase(0)
    first_phase(1)

    for load in loads[3:]:
        load.wait()
    count = cfg["count"]
    lengths = [lengths_ref[j] for j in range(count)]
    ends = []
    running = jnp.int32(0)
    for j in range(count):
        running = running + lengths[j]
        ends.append(running)

    values = tokens_ref[...].astype(jnp.float32)
    inverse = lax.rsqrt(jnp.mean(values * values, axis=-1, keepdims=True) + EPSILON)
    xn[...] = (values * inverse * gain_ref[...].astype(jnp.float32)).astype(jnp.bfloat16)
    kv_copy(1).wait()
    plain_v = jnp.dot(xn[...], wkv[1], preferred_element_type=jnp.float32).astype(jnp.bfloat16)
    vb0[0, lo] = plain_v[:half_rows]
    vb1[0, lo] = plain_v[half_rows:]

    def slot_of(position):
        prompt = jnp.int32(0)
        for j in range(count - 1):
            prompt = prompt + (ends[j] <= position).astype(jnp.int32)
        return place_ref[prompt_adapter_ref[prompt]]

    def second_copy(x, dest, source):
        _, _, stage, maps, piece, _ = groups[x]
        return pltpu.make_async_remote_copy(
            src_ref=stage.at[dest],
            dst_ref=maps.at[:, :, lanes(source, piece)],
            send_sem=s2_sem.at[x, dest],
            recv_sem=r2_sem.at[x, source],
            device_id=(dest, tp),
            device_id_type=MESH,
        )

    def second_phase(x):
        slab, part, stage, maps, piece, pieces = groups[x]

        @pl.when(me < pieces)
        def _():
            part[me] = slab[:, lanes(me, piece)]

            def first_wait(k, carry):
                first_copy(x, me, lax.rem(me + k, n)).wait_recv()
                return carry

            lax.fori_loop(1, n, first_wait, 0)

            def second_send(k, carry):
                dest = lax.rem(me + k, n)
                for u in range(units):
                    stage[dest, u] = part[slot_of((dest * units + u) * SHORT_LEN)]
                second_copy(x, dest, me).start()
                return carry

            lax.fori_loop(1, n, second_send, 0)
            for u in range(units):
                maps[u, :, lanes(me, piece)] = part[slot_of((me * units + u) * SHORT_LEN)]

    def second_arrival(x):
        def second_wait(k, carry):
            source = lax.rem(me + k, n)

            @pl.when(source < groups[x][5])
            def _():
                second_copy(x, me, source).wait_recv()

            return carry

        lax.fori_loop(1, n, second_wait, 0)

    xn_lo = lo + 1 - 2 * lax.rem(lo, 2)
    yn_lo = lax.rem(lo + 2, PLANE)
    dn_lo = PLANE - 1 - lo
    held = ((kb0, kb1), (vb0, vb1))

    def need(s, source, dest):
        if s == 0:
            return source < dest
        if s == back:
            return source > dest
        return source >= 0

    def z_copy(t, part, s):
        ref = held[t][part]
        return pltpu.make_async_remote_copy(
            src_ref=ref.at[s, lo],
            dst_ref=ref.at[s + 1, lo],
            send_sem=zs_sem.at[t, part, s],
            recv_sem=zr_sem.at[t, part, s + 1],
            device_id=(lax.rem(me + PLANE, n), tp),
            device_id_type=MESH,
        )

    def p_copy(t, kind, s, block, part, dest):
        ref = held[t][part]
        return pltpu.make_async_remote_copy(
            src_ref=ref.at[s, block],
            dst_ref=ref.at[s, block],
            send_sem=ps_sem.at[t, kind, s],
            recv_sem=pr_sem.at[t, kind, s],
            device_id=(hi * PLANE + dest, tp),
            device_id_type=MESH,
        )

    def plan(s, sender, x_of, y_of, d_of):
        return (
            (0, sender, 0, x_of, need(s, sender, x_of)),
            (1, sender, 1, x_of, need(s, sender, x_of) | need(s, sender, d_of)),
            (2, sender, 0, y_of, need(s, sender, y_of) | need(s, sender, d_of)),
            (3, sender, 1, y_of, need(s, sender, y_of)),
        )

    def relays(s):
        return (
            (4, yn_lo, 0, xn_lo, need(s, yn_lo, xn_lo)),
            (5, xn_lo, 1, yn_lo, need(s, xn_lo, yn_lo)),
        )

    def launch(t, s):
        if s < back:

            @pl.when((hi >= s) & (hi + 1 < planes))
            def _():
                z_copy(t, 0, s).start()
                z_copy(t, 1, s).start()

        first, second, third, fourth = plan(s, lo, xn_lo, yn_lo, dn_lo)
        for kind, block, part, dest, wanted in (second, third, first, fourth):

            @pl.when((hi >= s) & wanted)
            def _():
                p_copy(t, kind, s, block, part, dest).start()

    def arrive(t, s):
        from_x = plan(s, xn_lo, lo, dn_lo, yn_lo)[:2]
        from_y = plan(s, yn_lo, dn_lo, lo, xn_lo)[2:]
        for (kind, block, part, dest, wanted), relay in zip(
            (from_y[0], from_x[1], from_x[0], from_y[1]), relays(s) + (None, None)
        ):

            @pl.when((hi >= s) & wanted)
            def _():
                p_copy(t, kind, s, block, part, dest).wait_recv()

            if relay is not None:
                r_kind, r_block, r_part, r_dest, r_wanted = relay

                @pl.when((hi >= s) & r_wanted)
                def _():
                    p_copy(t, r_kind, s, r_block, r_part, r_dest).start()

    def diagonal(t, s):
        @pl.when((hi >= s) & need(s, dn_lo, lo))
        def _():
            p_copy(t, 4, s, dn_lo, 0, lo).wait_recv()
            p_copy(t, 5, s, dn_lo, 1, lo).wait_recv()

    def step(t, s):
        @pl.when(hi >= s)
        def _():
            z_copy(t, 0, s - 1).wait_recv()
            z_copy(t, 1, s - 1).wait_recv()

        launch(t, s)

    second_phase(0)
    launch(1, 0)

    if dseg > lw:
        xown[...] = jnp.zeros_like(xown)
    for k in range(tpn):

        @pl.when(tp == k)
        def _():
            xown[:, :lw] = xn[:, k * lw : (k + 1) * lw]

    dmaps[...] = jnp.zeros_like(dmaps)
    kv_copy(0).wait()
    plain_k[...] = jnp.dot(xn[...], wkv[0], preferred_element_type=jnp.float32)
    second_phase(1)

    row_pos = me * rows + lax.broadcasted_iota(jnp.int32, (rows, hw), 0)
    row_start = jnp.zeros((rows, hw), jnp.int32)
    for j in range(count):
        row_start = row_start + jnp.where(ends[j] <= row_pos, lengths[j], 0)
    angles = (row_pos - row_start).astype(jnp.float32) * freq_ref[...]
    sine = jnp.sin(angles)
    cos_t[...] = jnp.cos(angles)
    lane = lax.broadcasted_iota(jnp.int32, (rows, hw), 1)
    sin_t[...] = jnp.where(lane < hw // 2, -sine, sine)
    acc[...] = jnp.zeros_like(acc)
    accl[...] = jnp.zeros_like(accl)
    accd[...] = jnp.zeros_like(accd)

    def low_copy(x, k, source):
        return pltpu.make_async_remote_copy(
            src_ref=lowp.at[x],
            dst_ref=lowr.at[x, source],
            send_sem=sl_sem.at[x, k],
            recv_sem=rl_sem.at[x, source],
            device_id=(me, lax.rem(tp + k, tpn)),
            device_id_type=MESH,
        )

    def low_send(x, maps, parts):
        for u in range(units):
            for r in range(parts):
                dmaps[x, u, r * rank : (r + 1) * rank, :] = maps[u, :, r * dseg : (r + 1) * dseg]
            rows_u = slice(u * SHORT_LEN, (u + 1) * SHORT_LEN)
            lowp[x, rows_u, :] = nt_dot(xown[rows_u, :], dmaps[x, u])
        for k in range(1, tpn):
            low_copy(x, k, tp).start()

    def low_sum(x):
        low = lowp[x]
        for k in range(1, tpn):
            source = lax.rem(tp + k, tpn)
            low_copy(x, tpn - k, source).wait_recv()
            low = low + lowr[x, source]
        return low

    def increment(low, maps, start, width):
        return jnp.concatenate(
            [
                jnp.dot(
                    low[u * SHORT_LEN : (u + 1) * SHORT_LEN, :rank],
                    maps[u, :, pl.ds(start, width)],
                    preferred_element_type=jnp.float32,
                )
                for u in range(units)
            ],
            0,
        )

    def head(values, gain):
        inverse = lax.rsqrt(jnp.mean(values * values, axis=-1, keepdims=True) + EPSILON)
        values = values * inverse * gain
        return (values * cos_t[...] + pltpu.roll(values, hw // 2, 1) * sin_t[...]).astype(
            jnp.bfloat16
        )

    step(1, 1)
    arrive(1, 0)

    def q_product(c, carry):
        q_copy(c).wait()
        plain_q[c] = jnp.dot(xn[...], wq[c], preferred_element_type=jnp.float32)
        return carry

    lax.fori_loop(0, nkv, q_product, 0)

    second_arrival(0)
    low_send(0, maps_a, 2)
    low_kv = low_sum(0)
    kb0[0, lo, half_rows:, :rows] = low_kv.T[rank : 2 * rank, :].astype(jnp.bfloat16)
    kgain = kgain_ref[...].astype(jnp.float32)
    qgain = qgain_ref[...].astype(jnp.float32)
    k_raw = plain_k[...] + ADAPTER_SCALE * increment(
        low_kv.astype(jnp.bfloat16), maps_a, k_at, kvw
    )
    for k in range(nkv):
        cols = slice(k * hw, (k + 1) * hw)
        key = head(k_raw[:, cols], kgain)
        kb0[0, lo, :half_rows, cols] = key[:half_rows]
        kb1[0, lo, :, cols] = key[half_rows:]
    launch(0, 0)
    for s in range(2, back + 1):
        step(1, s)
        arrive(1, s - 1)

    second_arrival(1)
    low_send(1, maps_b, 1)
    low_q = low_sum(1).astype(jnp.bfloat16)

    def q_final(c, carry):
        start = pl.multiple_of(q_at + c * gw, 128)
        raw = plain_q[c] + ADAPTER_SCALE * increment(low_q, maps_b, start, gw)
        for g in range(group):
            qbuf[c, g * rows : (g + 1) * rows, :] = head(raw[:, g * hw : (g + 1) * hw], qgain)
        return carry

    lax.fori_loop(0, nkv, q_final, 0)

    factor = math.log2(math.e) / math.sqrt(hw)

    def attend(s, block, wanted):
        @pl.when((hi >= s) & wanted)
        def _():
            key_pos = ((hi - s) * PLANE + block) * rows + lax.broadcasted_iota(
                jnp.int32, (rows, rows), 1
            )
            query_pos = me * rows + lax.broadcasted_iota(jnp.int32, (rows, rows), 0)
            first = jnp.zeros((rows, rows), jnp.int32)
            for j in range(count):
                first = first + jnp.where(ends[j] <= query_pos, lengths[j], 0)
            bias = jnp.where((key_pos >= first) & (key_pos <= query_pos), 0.0, MASKED)
            bias = jnp.concatenate([bias] * group, 0)
            low_v = kb0[s, block, half_rows:, :rows]
            for k in range(nkv):
                cols = slice(k * hw, (k + 1) * hw)
                key = jnp.concatenate([kb0[s, block, :half_rows, cols], kb1[s, block, :, cols]], 0)
                value = jnp.concatenate([vb0[s, block, :, cols], vb1[s, block, :, cols]], 0)
                weights = jnp.exp2(nt_dot(qbuf[k], key) * factor + bias)
                accl[k] += weights
                weights = weights.astype(jnp.bfloat16)
                acc[k] += jnp.dot(weights, value, preferred_element_type=jnp.float32)
                accd[k] += nt_dot(weights, low_v)

    for s in range(back + 1):
        if s < back:
            step(0, s + 1)
        arrive(0, s)
        if s == back:
            arrive(1, s)
        if s == 0:
            attend(0, lo, lo >= 0)
        else:
            attend(s, lo, lo >= 0)
        attend(s, xn_lo, need(s, xn_lo, lo))
        attend(s, yn_lo, need(s, yn_lo, lo))
        if s >= 1:
            diagonal(1, s - 1)
            diagonal(0, s - 1)
            attend(s - 1, dn_lo, need(s - 1, dn_lo, lo))
    diagonal(1, back)
    diagonal(0, back)
    attend(back, dn_lo, need(back, dn_lo, lo))

    unit_of = lax.div(
        lax.rem(lax.broadcasted_iota(jnp.int32, (group * rows, hw), 0), rows), SHORT_LEN
    )
    for k in range(nkv):
        total = jnp.sum(accl[k], axis=-1, keepdims=True)
        low_mean = (accd[k] / total).astype(jnp.bfloat16)
        extra = jnp.zeros((group * rows, hw), jnp.float32)
        for u in range(units):
            up = maps_b[u, :, v_at + k * hw : v_at + (k + 1) * hw]
            extra = jnp.where(
                unit_of == u, jnp.dot(low_mean, up, preferred_element_type=jnp.float32), extra
            )
        result = (acc[k] / total + ADAPTER_SCALE * extra).astype(out_ref.dtype)
        for g in range(group):
            at = (k * group + g) * hw
            out_ref[:, at : at + hw] = result[g * rows : (g + 1) * rows, :]

    def drain(k, carry):
        dest = lax.rem(me + k, n)
        for x in range(2):

            @pl.when(dest < groups[x][5])
            def _():
                first_copy(x, dest, me).wait_send()

            @pl.when(me < groups[x][5])
            def _():
                second_copy(x, dest, me).wait_send()

        return carry

    lax.fori_loop(1, n, drain, 0)
    for x in range(2):
        for k in range(1, tpn):
            low_copy(x, k, tp).wait_send()
    for t in range(2):
        for s in range(back + 1):
            if s < back:

                @pl.when((hi >= s) & (hi + 1 < planes))
                def _():
                    z_copy(t, 0, s).wait_send()
                    z_copy(t, 1, s).wait_send()

            for kind, block, part, dest, wanted in (
                plan(s, lo, xn_lo, yn_lo, dn_lo) + relays(s)
            ):

                @pl.when((hi >= s) & wanted)
                def _():
                    p_copy(t, kind, s, block, part, dest).wait_send()


def on_device(
    n,
    tpn,
    tokens,
    input_norm_gain,
    query_weight,
    key_value_weight,
    query_head_gain,
    key_head_gain,
    adapter_down_maps,
    query_up_maps,
    key_value_up_maps,
    packed_lengths,
    adapter_per_prompt,
    adapter_place,
):
    rows, width = tokens.shape
    hw = query_head_gain.shape[0]
    nkv = key_value_weight.shape[2] // hw
    group = query_weight.shape[1] // hw // nkv
    rank, lw = query_up_maps.shape[1], adapter_down_maps.shape[2]
    units = rows // SHORT_LEN
    dseg = -(-lw // 128) * 128
    kvw, gw = nkv * hw, group * hw

    def pieces_of(used):
        piece = -(-(used // 128) // n) * 128
        return piece, -(-used // piece)

    piece_a, pieces_a = pieces_of(2 * dseg + kvw)
    piece_b, pieces_b = pieces_of(dseg + nkv * gw + kvw)
    back = n // 2 // PLANE
    cfg = dict(
        n=n,
        tpn=tpn,
        rows=rows,
        units=units,
        rank=rank,
        lw=lw,
        dseg=dseg,
        piece_a=piece_a,
        pieces_a=pieces_a,
        piece_b=piece_b,
        pieces_b=pieces_b,
        count=packed_lengths.shape[0],
        nkv=nkv,
        group=group,
        hw=hw,
    )
    powers = np.arange(hw // 2, dtype=np.float64) * (2.0 / hw)
    frequency = (THETA ** (-powers)).astype(np.float32)
    frequency = jnp.asarray(np.concatenate([frequency, frequency])[None, :])
    vmem = pl.BlockSpec(memory_space=pltpu.VMEM)
    hbm = pl.BlockSpec(memory_space=pltpu.HBM)
    bf, f32 = jnp.bfloat16, jnp.float32
    dma = pltpu.SemaphoreType.DMA
    call = pl.pallas_call(
        functools.partial(fused_kernel, cfg),
        out_shape=jax.ShapeDtypeStruct((rows, nkv * gw), bf),
        in_specs=[hbm] * 13,
        out_specs=vmem,
        scratch_shapes=[
            pltpu.SMEM(packed_lengths.shape, jnp.int32),
            pltpu.SMEM(adapter_per_prompt.shape, jnp.int32),
            pltpu.SMEM(adapter_place.shape, jnp.int32),
            pltpu.VMEM((rows, width), bf),
            pltpu.VMEM((1, width), bf),
            pltpu.VMEM((1, hw), bf),
            pltpu.VMEM((1, hw), bf),
            pltpu.VMEM((1, hw), f32),
            pltpu.VMEM(adapter_down_maps.shape, bf),
            pltpu.VMEM(query_up_maps.shape, bf),
            pltpu.VMEM(key_value_up_maps.shape, bf),
            pltpu.VMEM((nkv, width, gw), bf),
            pltpu.VMEM((2, width, kvw), bf),
            pltpu.VMEM((rows, width), bf),
            pltpu.VMEM((rows, dseg), bf),
            pltpu.VMEM((rank, pieces_a * piece_a), bf),
            pltpu.VMEM((rank, pieces_b * piece_b), bf),
            pltpu.VMEM((n, rank, piece_a), bf),
            pltpu.VMEM((n, rank, piece_b), bf),
            pltpu.VMEM((n, units, rank, piece_a), bf),
            pltpu.VMEM((n, units, rank, piece_b), bf),
            pltpu.VMEM((units, rank, pieces_a * piece_a), bf),
            pltpu.VMEM((units, rank, pieces_b * piece_b), bf),
            pltpu.VMEM((2, units, 128, dseg), bf),
            pltpu.VMEM((2, rows, 128), f32),
            pltpu.VMEM((2, tpn, rows, 128), f32),
            pltpu.VMEM((nkv, rows, gw), f32),
            pltpu.VMEM((rows, kvw), f32),
            pltpu.VMEM((nkv, group * rows, hw), bf),
            pltpu.VMEM((back + 1, PLANE, rows // 2 + rank, kvw), bf),
            pltpu.VMEM((back + 1, PLANE, rows // 2, kvw), bf),
            pltpu.VMEM((back + 1, PLANE, rows // 2, kvw), bf),
            pltpu.VMEM((back + 1, PLANE, rows // 2, kvw), bf),
            pltpu.VMEM((nkv, group * rows, hw), f32),
            pltpu.VMEM((nkv, group * rows, rows), f32),
            pltpu.VMEM((nkv, group * rows, rank), f32),
            pltpu.VMEM((rows, hw), f32),
            pltpu.VMEM((rows, hw), f32),
            dma((11,)),
            dma((nkv,)),
            dma((2,)),
            dma((2, n)),
            dma((2, n)),
            dma((2, n)),
            dma((2, n)),
            dma((2, tpn)),
            dma((2, tpn)),
            dma((2, 2, back + 1)),
            dma((2, 2, back + 1)),
            dma((2, 6, back + 1)),
            dma((2, 6, back + 1)),
        ],
        compiler_params=pltpu.CompilerParams(
            collective_id=0, has_side_effects=True, vmem_limit_bytes=56 << 20
        ),
    )
    return call(
        packed_lengths,
        adapter_per_prompt,
        adapter_place,
        tokens,
        input_norm_gain.reshape(1, -1),
        query_head_gain.reshape(1, -1),
        key_head_gain.reshape(1, -1),
        frequency,
        adapter_down_maps,
        query_up_maps,
        key_value_up_maps,
        query_weight,
        key_value_weight,
    )


def solution(mesh):
    in_specs = (
        P("req", None),
        P(),
        P(None, "tp"),
        P(None, None, "tp"),
        P(),
        P(),
        P("req", None, "tp"),
        P("req", None, "tp"),
        P("req", None, None, "tp"),
        P(),
        P(),
        P(),
    )
    body = functools.partial(on_device, mesh.shape["req"], mesh.shape["tp"])
    return jax.shard_map(
        body, mesh=mesh, in_specs=in_specs, out_specs=P("req", "tp"), check_vma=False
    )
```

time: 64.3 us -> 53.8 us (0.84)
  local copies, waits for them, and re-layouts: 9 us -> 3.18 us
  Pallas kernels: 54.8 us -> 50.4 us
    unnamed x21 -> x1, local copies, waits for them, and re-layouts: 8.31 us -> 1.88 us
    pallas_call x1, Pallas kernels: 54.8 us -> 50.4 us  [on_device(): call(packed_lengths, adapter_per_prompt, adapter_place, tokens, input_nor...]
where the time goes in v2:
time: 53.8 us; the launch traced here: 53.6 us
  Pallas kernels  50.4 us (94%)
  local copies, waits for them, and re-layouts  3.18 us (6%)
    pallas_call x1, Pallas kernels, on_device(): call(packed_lengths, adapter_per_prompt, adapter_place, tokens, input_nor...  50.4 us
    unnamed x1, local copies, waits for them, and re-layouts  1.88 us
    reshape x1, local copies, waits for them, and re-layouts, on_device(): input_norm_gain.reshape(1, -1)  1.3 us

profile of v2, /device:TPU:16, one launch (start us, length us, event | category | flops | bytes accessed | tf_op | source)
XLA Modules:
  0.0 53.6 jit_solution(16787729767009284988)
XLA Ops:
  0.0 1.3 %reshape.9.gain_hbm = bf16[1,2560]{1,0:T(2,128)(2,1)} reshape(bf16[2560]{0:T(1024)(128)(2,1)} %param.14) | data formatting | bytes 10240 | tf_op jit(solution)/shard_map/reshape | solution.py:706
  1.3 50.4 %shard_map.127 = bf16[128,2048]{1,0:T(8,128)(2,1)} custom-call(s32[4]{0:T(128)} %lengths_hbm.1, s32[4]{0:T(128)} %prompt_adapter_hbm.1, s32[16]{0:T(128)} %place_hbm.1, bf16[128,2560]{1,0:T(8,128)(2,1)} %tokens_hbm.1, bf16[1,2560]{1,0:T(2,128)(2,1)} %reshape.9.gain_hbm, bf16[1,128]{1,0:T(2,128)(2,1)} %bitcast.2, bf16[1,128]{1,0:T(2,128)(2,1)} %bitcast.3, ...), custom_call_target="tpu_custom_call" | custom-call | tf_op jit(solution)/shard_map/pallas_call | solution.py:701
  51.7 1.9 %copy.15 = bf16[128,2048]{1,0:T(8,128)(2,1)} copy(bf16[128,2048]{1,0:T(8,128)(2,1)} %shard_map.127) | data formatting | bytes 1048576

commit v3 on v2

--- a/solution.py
+++ b/solution.py
@@ -210,7 +210,7 @@
 
     values = tokens_ref[...].astype(jnp.float32)
     inverse = lax.rsqrt(jnp.mean(values * values, axis=-1, keepdims=True) + EPSILON)
-    xn[...] = (values * inverse * gain_ref[...].astype(jnp.float32)).astype(jnp.bfloat16)
+    xn[...] = (values * inverse * gain_ref[...].astype(jnp.float32).reshape(1, -1)).astype(jnp.bfloat16)
     kv_copy(1).wait()
     plain_v = jnp.dot(xn[...], wkv[1], preferred_element_type=jnp.float32).astype(jnp.bfloat16)
     vb0[0, lo] = plain_v[:half_rows]
@@ -646,7 +646,7 @@
             pltpu.SMEM(adapter_per_prompt.shape, jnp.int32),
             pltpu.SMEM(adapter_place.shape, jnp.int32),
             pltpu.VMEM((rows, width), bf),
-            pltpu.VMEM((1, width), bf),
+            pltpu.VMEM((width,), bf),
             pltpu.VMEM((1, hw), bf),
             pltpu.VMEM((1, hw), bf),
             pltpu.VMEM((1, hw), f32),
@@ -703,7 +703,7 @@
         adapter_per_prompt,
         adapter_place,
         tokens,
-        input_norm_gain.reshape(1, -1),
+        input_norm_gain,
         query_head_gain.reshape(1, -1),
         key_head_gain.reshape(1, -1),
         frequency,

time: 53.8 us -> 52.4 us (0.974)
  local copies, waits for them, and re-layouts: 3.18 us -> 1.88 us
    reshape x1 -> x0, local copies, waits for them, and re-layouts: 1.3 us -> none  [on_device(): input_norm_gain.reshape(1, -1)]
where the time goes in v3:
time: 52.4 us; the launch traced here: 52.3 us
  Pallas kernels  50.4 us (96%)
  local copies, waits for them, and re-layouts  1.88 us (4%)
    pallas_call x1, Pallas kernels, on_device(): call(packed_lengths, adapter_per_prompt, adapter_place, tokens, input_nor...  50.4 us
    unnamed x1, local copies, waits for them, and re-layouts  1.88 us

profile of v3, /device:TPU:16, one launch (start us, length us, event | category | flops | bytes accessed | tf_op | source)
XLA Modules:
  0.0 52.3 jit_solution(6791103623963128720)
XLA Ops:
  0.0 50.4 %shard_map.127 = bf16[128,2048]{1,0:T(8,128)(2,1)} custom-call(s32[4]{0:T(128)} %lengths_hbm.1, s32[4]{0:T(128)} %prompt_adapter_hbm.1, s32[16]{0:T(128)} %place_hbm.1, bf16[128,2560]{1,0:T(8,128)(2,1)} %tokens_hbm.1, bf16[2560]{0:T(1024)(128)(2,1)} %gain_hbm.1, bf16[1,128]{1,0:T(2,128)(2,1)} %bitcast.2, bf16[1,128]{1,0:T(2,128)(2,1)} %bitcast.3, ...), custom_call_target="tpu_custom_call" | custom-call | tf_op jit(solution)/shard_map/pallas_call | solution.py:701
  50.4 1.9 %copy.15 = bf16[128,2048]{1,0:T(8,128)(2,1)} copy(bf16[128,2048]{1,0:T(8,128)(2,1)} %shard_map.127) | data formatting | bytes 1048576
